TPU v7x, 32 devices: a whole 2x2x4 slice. The times are simulated.
32 devices in a mesh: grp: 2 (over y), ka: 4 (over z), vib: 2 (over core), fin: 2 (over x).
Axes of the slice: x: 2, y: 2, z: 4, core: 2. Of those that a mesh axis runs over, the one named last changes fastest.
Arguments:
- moments: bfloat16 [2, 2048, 2048], P(None, 'vib'), may hold values from -0.125 to 0.125
- initial_vectors: bfloat16 [8, 2048, 2048], P('ka', 'vib', 'grp'), parts along dimension 2, may hold values from -6 to 6
- final_vectors: bfloat16 [8, 2048, 1024], P('ka', 'vib', ('grp', 'fin')), parts along dimension 2, may hold values from -0.046875 to 0.046875
- basis_counts: int32 [16], P(('grp', 'ka')), parts along dimension 0, may hold values from 512 to 2048
Outputs:
- strengths: float32 [2048, 512], P(('grp', 'ka', 'vib'), 'fin'), parts along dimension 0
There are 2 independent parts, one for each index of `grp`. A program takes and returns all parts, laid end to end along the dimension named above; an argument that names none is the same for every part. Nothing has to cross between parts.
All inputs are finite; a program needn't handle non-finite values.
Results may differ from a plain program's by a relative error of at most 0.0003.
Values may be sent and summed in bfloat16 or wider, within the bound.
A program may use at most 64 MiB of HBM per device.

v0:
```python
import jax
import jax.numpy as jnp
from jax import lax
from jax.sharding import PartitionSpec as P

JQ = 30


def extended(shard, sides, width):
    for axis, dim in sides:
        size, length = (lax.axis_size(axis), shard.shape[dim])
        up = [(i, (i + 1) % size) for i in range(size - 1)]
        down = [(j, i) for i, j in up]
        last = lax.slice_in_dim(shard, length - width, length, axis=dim)
        initial = lax.slice_in_dim(shard, 0, width, axis=dim)
        before = lax.ppermute(last, axis, up)
        after = lax.ppermute(initial, axis, down)
        shard = jnp.concatenate([before, shard, after], axis=dim)
    return shard


def coefficients(first_block, count, total_blocks):
    jsquare = float(JQ * (JQ + 1))
    norm_j = jnp.sqrt(jnp.float32(jsquare))
    k_index = first_block + jnp.arange(count, dtype=jnp.int32) - total_blocks // 2
    k_value = k_index.astype(jnp.float32)
    coef_same = k_value / norm_j
    coef_upper = 0.5 * jnp.sqrt(jsquare - k_value * (k_value + 1.0)) / norm_j
    coef_lower = -0.5 * jnp.sqrt(jsquare - k_value * (k_value - 1.0)) / norm_j
    return (coef_same, coef_upper, coef_lower)


def on_device(moments, initial_vectors, final_vectors, basis_counts):
    kblocks, vib_rows, states = initial_vectors.shape
    total_blocks = kblocks * lax.axis_size("ka")
    first_block = lax.axis_index("ka") * kblocks
    row_index = lax.axis_index("vib") * vib_rows + jnp.arange(vib_rows, dtype=jnp.int32)
    keep_mask = row_index[None, :] < basis_counts[:, None]
    initial_live = jnp.where(
        keep_mask[:, :, None], initial_vectors, jnp.zeros((), initial_vectors.dtype)
    )
    final_live = jnp.where(keep_mask[:, :, None], final_vectors, jnp.zeros((), final_vectors.dtype))
    final_whole = lax.all_gather(final_live, "vib", axis=1, tiled=True)
    images = jnp.einsum("cvw,kwf->vkcf", moments, final_whole, preferred_element_type=jnp.float32)
    widened = extended(images[:, :, 1], (("ka", 1),), 1)
    ext_same, ext_upper, ext_lower = coefficients(first_block - 1, kblocks + 2, total_blocks)
    coef_same = ext_same[1:-1]
    combined = (
        coef_same[None, :, None] * images[:, :, 0]
        + ext_upper[:-2][None, :, None] * widened[:, :-2]
        + ext_lower[2:][None, :, None] * widened[:, 2:]
    )
    amplitude = jnp.einsum(
        "kvi,vkf->if", initial_live.astype(jnp.float32), combined, precision=lax.Precision.HIGHEST
    )
    summed = lax.psum(amplitude, ("ka", "vib"))
    row_share = states // lax.axis_size(("ka", "vib"))
    amplitude = lax.dynamic_slice_in_dim(
        summed, lax.axis_index(("ka", "vib")) * row_share, row_share, 0
    )
    return amplitude * amplitude


def solution(mesh):
    in_specs = (
        P(None, "vib", None),
        P("ka", "vib", "grp"),
        P("ka", "vib", ("grp", "fin")),
        P(("grp", "ka")),
    )
    out_specs = P(("grp", "ka", "vib"), "fin")
    return jax.shard_map(
        on_device, mesh=mesh, in_specs=in_specs, out_specs=out_specs, check_vma=False
    )
```

profile of v0, /device:TPU:0, one launch (start us, length us, event | category | flops | bytes accessed | tf_op | source)
XLA Modules:
  0.0 141.9 jit_solution(8668482068040856457)
XLA Ops:
  6.5 0.0 copy-start.1
  6.5 0.0 all-gather.2.cloned.1.call-start
  6.5 1.5 %copy.5 = bf16[2,1024,256]{1,2,0:T(8,128)(2,1)S(1)} copy(bf16[2,1024,256]{2,1,0:T(8,128)(2,1)} %param.6) | data formatting | bytes 2097152 | tf_op args[2]
  8.0 0.0 copy-done.1
  8.0 0.1 broadcast_compare_fusion
  8.1 1.1 broadcast_select_fusion
  9.2 0.0 all-gather.2.cloned.1.call-update
  9.2 0.0 all-reduce.2.cloned.1.call-start
  9.3 13.4 %all-gather.2.cloned.1.call-done = bf16[2,2048,256]{1,2,0:T(8,128)(2,1)} async-done(((bf16[2,1024,256]{1,2,0:T(8,128)(2,1)}), bf16[2,2048,256]{1,2,0:T(8,128)(2,1)}) %all-gather.2.cloned.1.call-update) | async-done | bytes 2097168 | tf_op jit(solution)/shard_map/all_gather | solution.py:43
  22.7 7.6 %fusion.5 = f32[1024,2,2,256]{0,3,2,1:T(8,128)S(1)} fusion(bf16[2,1024,2048]{2,1,0:T(8,128)(2,1)} %param.4, bf16[2,2048,256]{1,2,0:T(8,128)(2,1)} %all-gather.2.cloned.1.call-done), kind=kOutput, calls=%fused_computation.5 | convolution fusion | flops 4294967296 | bytes 14680064 | tf_op jit(solution)/shard_map/cvw,kwf->vkcf/dot_general | solution.py:44
  30.3 0.0 copy-start
  30.3 0.1 slice_bitcast_fusion
  30.5 1.8 %copy-done = f32[1024,2,2,256]{0,3,2,1:T(8,128)} copy-done((f32[1024,2,2,256]{0,3,2,1:T(8,128)}, f32[1024,2,2,256]{0,3,2,1:T(8,128)S(1)}, u32[]{:S(2)}) %copy-start) | copy-done | bytes 4194328
  32.3 1.2 fusion.36
  33.4 4.7 %collective-permute-start = (f32[1024,1,256]{0,2,1:T(8,128)}, f32[1024,1,256]{0,2,1:T(8,128)}, u32[]{:S(2)}, u32[]{:S(2)}) collective-permute-start(f32[1024,1,256]{0,2,1:T(8,128)} %get-tuple-element.5), channel_id=1, source_target_pairs={{0,4},{4,8},{8,12},{1,5},{5,9},{9,13},{2,6},{6,10},{10,14},{3,7},{... | collective-permute-start | bytes 3145736 | tf_op jit(solution)/shard_map/ppermute | solution.py:16
  38.1 1.3 collective-permute-start.1
  39.4 0.1 slice.35
  39.5 0.1 slice.29
  39.6 20.7 %collective-permute-done = f32[1024,1,256]{0,2,1:T(8,128)} collective-permute-done((f32[1024,1,256]{0,2,1:T(8,128)}, f32[1024,1,256]{0,2,1:T(8,128)}, u32[]{:S(2)}, u32[]{:S(2)}) %collective-permute-start) | collective-permute-done | bytes 1048608 | tf_op jit(solution)/shard_map/ppermute | solution.py:16
  60.3 4.9 %collective-permute-done.1 = f32[1024,1,256]{0,2,1:T(8,128)} collective-permute-done((f32[1024,1,256]{0,2,1:T(8,128)S(1)}, f32[1024,1,256]{0,2,1:T(8,128)}, u32[]{:S(2)}, u32[]{:S(2)}) %collective-permute-start.1) | collective-permute-done | bytes 1048608 | tf_op jit(solution)/shard_map/ppermute | solution.py:17
  65.2 9.9 %fusion.20 = f32[1024,256]{1,0:T(8,128)} fusion(f32[1024,1,256]{0,2,1:T(8,128)} %collective-permute-done.1, f32[1024,2,256]{0,2,1:T(8,128)S(1)} %slice_bitcast_fusion, f32[1024,1,256]{0,2,1:T(8,128)} %collective-permute-done, f32[1024,2,2,256]{0,3,2,1:T(8,128)} %copy-done, bf16[2,1024,1024]{2,1,0:T(8,128)(2,1)} %param.5, ...), kind=kOutput, calls=%fused_computation.19 | convolution fusion | flops 6448218112 | bytes 11536408 | tf_op jit(solution)/shard_map/kvi,vkf->if/dot_general | solution.py:53
  75.0 0.0 all-reduce.2.cloned.1.call-update
  75.1 58.5 %all-reduce.2.cloned.1.call-done = f32[1024,256]{1,0:T(8,128)} async-done(((f32[1024,256]{1,0:T(8,128)}), f32[1024,256]{1,0:T(8,128)}) %all-reduce.2.cloned.1.call-update) | async-done | bytes 1048592 | tf_op jit(solution)/shard_map/psum | solution.py:56
  133.5 1.6 %dynamic-slice_multiply_fusion = f32[128,256]{1,0:T(8,128)} fusion(f32[1024,256]{1,0:T(8,128)} %all-reduce.2.cloned.1.call-done, s32[]{:T(128)S(6)} %select_n.13), kind=kLoop, calls=%fused_computation.24 | loop fusion | flops 32768 | bytes 262148 | tf_op jit(solution)/shard_map/mul | solution.py:61
  (3 shorter events, 0.0 us)
Async XLA Ops:
  6.5 1.5 %copy-start.1 = (s32[2]{0:T(128)S(1)}, s32[2]{0:T(128)}, u32[]{:S(2)}) copy-start(s32[2]{0:T(128)} %param.7) | copy-start | bytes 28
  6.5 16.1 %all-gather.2.cloned.1.call-start = ((), (), s32[]{:S(2)}) async-start(), calls=%async_computation | async-start | bytes 3145728 | tf_op jit(solution)/shard_map/all_gather | solution.py:43
  9.2 124.3 %all-reduce.2.cloned.1.call-start = ((), (), s32[]{:S(2)}) async-start(), calls=%async_computation.1 | async-start | bytes 2097152 | tf_op jit(solution)/shard_map/psum | solution.py:56
  30.3 1.9 %copy-start = (f32[1024,2,2,256]{0,3,2,1:T(8,128)}, f32[1024,2,2,256]{0,3,2,1:T(8,128)S(1)}, u32[]{:S(2)}) copy-start(f32[1024,2,2,256]{0,3,2,1:T(8,128)S(1)} %fusion.5) | copy-start | bytes 12582916
  33.4 26.8 %collective-permute-start = (f32[1024,1,256]{0,2,1:T(8,128)}, f32[1024,1,256]{0,2,1:T(8,128)}, u32[]{:S(2)}, u32[]{:S(2)}) collective-permute-start(f32[1024,1,256]{0,2,1:T(8,128)} %get-tuple-element.5), channel_id=1, source_target_pairs={{0,4},{4,8},{8,12},{1,5},{5,9},{9,13},{2,6},{6,10},{10,14},{3,7},{... | collective-permute-start | bytes 3145736 | tf_op jit(solution)/shard_map/ppermute | solution.py:16
  38.1 27.1 %collective-permute-start.1 = (f32[1024,1,256]{0,2,1:T(8,128)S(1)}, f32[1024,1,256]{0,2,1:T(8,128)}, u32[]{:S(2)}, u32[]{:S(2)}) collective-permute-start(f32[1024,1,256]{0,2,1:T(8,128)S(1)} %get-tuple-element.6), channel_id=1, source_target_pairs={{4,0},{8,4},{12,8},{5,1},{9,5},{13,9},{6,2},{10,6},{14,10},{7,3},{... | collective-permute-start | bytes 3145736 | tf_op jit(solution)/shard_map/ppermute | solution.py:17
Sparse Core Ops, SparseCore 0:
  9.3 13.2 all-gather.1
  75.2 58.2 all-reduce.1
where the time goes:
time: 142 us
  waiting for transfers between devices  97.5 us (69%)
  matrix products  17.5 us (12%)
  between operations  13.5 us (10%)
  starting transfers between devices  5.98 us (4%)
  local copies, waits for them, and re-layouts  4.75 us (3%)
  other arithmetic  2.73 us (2%)
    psum x1, waiting for transfers between devices, on_device(): summed = lax.psum(amplitude, ('ka', 'vib'))  58.5 us
    ppermute x1, waiting for transfers between devices, extended(): before = lax.ppermute(last, axis, up)  20.7 us
    all_gather x1, waiting for transfers between devices, on_device(): final_whole = lax.all_gather(final_live, 'vib', axis=1, tiled=True)  13.4 us
    dot_general x1, matrix products, on_device(): jnp.einsum('kvi,vkf->if', initial_live.astype(jnp.float32), combined, pre...  9.88 us
    dot_general x1, matrix products, on_device(): jnp.einsum('cvw,kwf->vkcf', moments, final_whole, preferred_element_type=...  7.63 us
    ppermute x1, waiting for transfers between devices, extended(): after = lax.ppermute(initial, axis, down)  4.89 us
    ppermute x1, starting transfers between devices, extended(): before = lax.ppermute(last, axis, up)  4.65 us
    unnamed x5, local copies, waits for them, and re-layouts  3.29 us
  transfers between devices with their start and end apart: 4, of which 4 were waited for; matrix products, arithmetic and copies ran while one was open for 0% of the time, Pallas kernels for 0%

commit v1 on v0

v1 whole, which is shorter than its diff:
```python
import functools

import jax
import jax.numpy as jnp
from jax import lax
from jax.experimental import pallas as pl
from jax.experimental.pallas import tpu as pltpu
from jax.sharding import PartitionSpec as P

JQ = 30
MESH = pl.DeviceIdType.MESH
F32 = jnp.float32
BF16 = jnp.bfloat16


def coefficient_rows(index, width):
    value = jnp.full((1, width), index, jnp.int32).astype(F32)
    jsquare = float(JQ * (JQ + 1))
    norm_j = jnp.sqrt(jnp.full((1, width), jsquare, F32))
    same = value / norm_j
    upper = 0.5 * jnp.sqrt(jsquare - value * (value + 1.0)) / norm_j
    lower = -0.5 * jnp.sqrt(jsquare - value * (value - 1.0)) / norm_j
    return same, upper, lower


def kernel(
    n_ka, chunks, counts_ref, moments_hbm, initial_hbm, final_hbm, out_ref,
    mom, ini, raw, fin, comb, split, amp, part, zsend, zrecv,
    mom_sem, ini_sem, raw_sem, own_send, own_recv, z_send, z_recv,
    fwd_send, fwd_recv, part_send, part_recv, out_send, out_recv,
):
    kblocks, rows, width = raw.shape
    states = ini.shape[2]
    share = out_ref.shape[0]
    whole = mom.shape[2]
    total_blocks = kblocks * n_ka
    a = lax.axis_index("ka")
    b = lax.axis_index("vib")
    other = 1 - b
    first = a * kblocks - total_blocks // 2

    get_final = pltpu.make_async_copy(final_hbm, raw, raw_sem)
    get_final.start()
    tile = mom.shape[1] // mom_sem.shape[1]
    get_moments = []
    for t in range(mom_sem.shape[1]):
        for c in range(2):
            get_moments.append(
                pltpu.make_async_copy(
                    moments_hbm.at[c, pl.ds(t * tile, tile)],
                    mom.at[c, pl.ds(t * tile, tile)],
                    mom_sem.at[c, t],
                )
            )
            get_moments[-1].start()
    get_initial = pltpu.make_async_copy(initial_hbm, ini, ini_sem)
    get_initial.start()

    barrier = pltpu.get_barrier_semaphore()
    pl.semaphore_signal(barrier, inc=1, device_id={"vib": other}, device_id_type=MESH)
    for d in range(1, n_ka):
        pl.semaphore_signal(
            barrier, inc=1, device_id={"ka": lax.rem(a + d, n_ka)}, device_id_type=MESH
        )

    get_final.wait()
    own_rows = pl.ds(pl.multiple_of(b * rows, rows), rows)
    row_index = lax.broadcasted_iota(jnp.int32, (rows, width), 0) + b * rows
    for k in range(kblocks):
        live = row_index < counts_ref[k]
        fin[1 + k, own_rows, :] = jnp.where(live, raw[k].astype(F32), 0.0).astype(BF16)

    has_up = a < n_ka - 1
    has_down = a > 0
    pl.semaphore_wait(barrier, n_ka)

    step = rows // chunks

    def at(core, j):
        return pl.ds(pl.multiple_of(core * rows + j * step, step), step)

    def z_copy(side, j):
        src, dst, to = (2, 0, a + 1) if side == 0 else (1, 3, a - 1)
        return pltpu.make_async_remote_copy(
            src_ref=fin.at[src, at(b, j)],
            dst_ref=fin.at[dst, at(b, j)],
            send_sem=z_send.at[side, j],
            recv_sem=z_recv.at[side, j],
            device_id={"ka": to},
            device_id_type=MESH,
        )

    def forward(side, j):
        slot = 0 if side == 0 else 3
        return pltpu.make_async_remote_copy(
            src_ref=fin.at[slot, at(b, j)],
            dst_ref=fin.at[slot, at(b, j)],
            send_sem=fwd_send.at[side, j],
            recv_sem=fwd_recv.at[side, j],
            device_id={"vib": other},
            device_id_type=MESH,
        )

    sends = (has_up, has_down)
    takes = (has_down, has_up)
    for j in range(chunks):
        for side in range(2):
            @pl.when(sends[side])
            def _():
                z_copy(side, j).start()
    own = pltpu.make_async_remote_copy(
        src_ref=fin.at[pl.ds(1, kblocks), own_rows],
        dst_ref=fin.at[pl.ds(1, kblocks), own_rows],
        send_sem=own_send,
        recv_sem=own_recv,
        device_id={"vib": other},
        device_id_type=MESH,
    )
    own.start()
    for side in range(2):
        @pl.when(jnp.logical_not(takes[side]))
        def _():
            fin[3 * side] = jnp.zeros((whole, width), BF16)

    same0, upper0, _ = coefficient_rows(first, width)
    same1, _, lower1 = coefficient_rows(first + 1, width)
    _, upper_below, _ = coefficient_rows(first - 1, width)
    _, _, lower_above = coefficient_rows(first + 2, width)

    own.wait_recv()
    for t in range(mom_sem.shape[1]):
        get_moments[2 * t].wait()
        get_moments[2 * t + 1].wait()
        span = pl.ds(t * tile, tile)
        z_part = functools.partial(jnp.dot, mom[0, span, :], preferred_element_type=F32)
        x_part = functools.partial(jnp.dot, mom[1, span, :], preferred_element_type=F32)
        comb[0, span, :] = same0 * z_part(fin[1]) + lower1 * x_part(fin[2])
        comb[1, span, :] = same1 * z_part(fin[2]) + upper0 * x_part(fin[1])

    edge = (upper_below, lower_above)

    def take(side, core, j):
        piece = fin[3 * side, at(core, j), :]
        cols = pl.ds(pl.multiple_of(core * rows + j * step, step), step)
        comb[side] = comb[side] + edge[side] * jnp.dot(
            mom[1, :, cols], piece, preferred_element_type=F32
        )

    for j in range(chunks):
        for side in range(2):
            @pl.when(takes[side])
            def _():
                z_copy(side, j).wait_recv()
                forward(side, j).start()
        for side in range(2):
            take(side, b, j)
        for side in range(2):
            @pl.when(takes[side])
            def _():
                forward(side, j).wait_recv()
        for side in range(2):
            take(side, other, j)

    block = min(256, rows)
    lane_index = lax.broadcasted_iota(jnp.int32, (width, block), 1) + b * rows
    for k in range(kblocks):
        for t in range(rows // block):
            turned = comb[k, pl.ds(t * block, block), :].T
            turned = jnp.where(lane_index + t * block < counts_ref[k], turned, 0.0)
            high = turned.astype(BF16)
            low = (turned - high.astype(F32)).astype(BF16)
            split[k, pl.ds(0, width), pl.ds(t * block, block)] = high
            split[k, pl.ds(width, width), pl.ds(t * block, block)] = low

    get_initial.wait()
    lanes = min(256, states)
    n_blocks = states // lanes
    targets = lanes // (2 * share)
    own_block = a // targets if targets > 1 else a

    def block_of(s):
        return lax.rem(own_block + 1 + s, n_blocks)

    def part_copy(s):
        span = pl.ds(pl.multiple_of(block_of(s) * (targets * share), targets * share), targets * share)
        return pltpu.make_async_remote_copy(
            src_ref=amp.at[other, span],
            dst_ref=part.at[span],
            send_sem=part_send.at[s],
            recv_sem=part_recv.at[s],
            device_id={"vib": other},
            device_id_type=MESH,
        )

    def out_copy(target, slot):
        return pltpu.make_async_remote_copy(
            src_ref=zsend.at[slot],
            dst_ref=zrecv.at[a],
            send_sem=out_send.at[slot],
            recv_sem=out_recv.at[a],
            device_id={"ka": target},
            device_id_type=MESH,
        )

    def finish(s):
        part_copy(s).wait_recv()
        for j in range(targets):
            target = block_of(s) * targets + j
            span = pl.ds(pl.multiple_of(target * share, share), share)
            slot = s * targets + j
            value = amp[b, span, :] + part[span, :]
            zsend[slot] = value

            @pl.when(target == a)
            def _():
                out_ref[...] = value

            @pl.when(target != a)
            def _():
                out_copy(target, slot).start()

    for s in range(n_blocks):
        cols = pl.ds(pl.multiple_of(block_of(s) * lanes, lanes), lanes)
        both = jnp.dot(split[0], ini[0, :, cols], preferred_element_type=F32)
        for k in range(1, kblocks):
            both = both + jnp.dot(split[k], ini[k, :, cols], preferred_element_type=F32)
        value = (both[:width] + both[width:]).T
        for j in range(targets):
            for core in range(2):
                low = (j * 2 + core) * share
                target = block_of(s) * targets + j
                amp[core, pl.ds(pl.multiple_of(target * share, share), share), :] = value[
                    low : low + share
                ]
        part_copy(s).start()
        if s > 0:
            finish(s - 1)
    finish(n_blocks - 1)

    for d in range(1, n_ka):
        sender = lax.rem(a + d, n_ka)
        pltpu.make_async_remote_copy(
            src_ref=zsend.at[0],
            dst_ref=zrecv.at[sender],
            send_sem=out_send.at[0],
            recv_sem=out_recv.at[sender],
            device_id={"ka": sender},
            device_id_type=MESH,
        ).wait_recv()
        out_ref[...] = out_ref[...] + zrecv[sender]

    own.wait_send()
    for j in range(chunks):
        for side in range(2):
            @pl.when(sends[side])
            def _():
                z_copy(side, j).wait_send()

            @pl.when(takes[side])
            def _():
                forward(side, j).wait_send()
    for s in range(n_blocks):
        part_copy(s).wait_send()
        for j in range(targets):
            target = block_of(s) * targets + j

            @pl.when(target != a)
            def _():
                out_copy(target, s * targets + j).wait_send()


def on_device(n_ka, moments, initial_vectors, final_vectors, basis_counts):
    kblocks, rows, states = initial_vectors.shape
    width = final_vectors.shape[2]
    whole = moments.shape[2]
    share = states // (2 * n_ka)
    chunks = 4
    tiles = 2
    dma = pltpu.SemaphoreType.DMA
    n_blocks = states // min(256, states)
    amplitude = pl.pallas_call(
        functools.partial(kernel, n_ka, chunks),
        out_shape=jax.ShapeDtypeStruct((share, width), F32),
        in_specs=[pl.BlockSpec(memory_space=pltpu.SMEM)]
        + [pl.BlockSpec(memory_space=pl.ANY)] * 3,
        out_specs=pl.BlockSpec(memory_space=pltpu.VMEM),
        scratch_shapes=[
            pltpu.VMEM(moments.shape, BF16),
            pltpu.VMEM(initial_vectors.shape, BF16),
            pltpu.VMEM(final_vectors.shape, BF16),
            pltpu.VMEM((kblocks + 2, whole, width), BF16),
            pltpu.VMEM((kblocks, rows, width), F32),
            pltpu.VMEM((kblocks, 2 * width, rows), BF16),
            pltpu.VMEM((2, n_ka * share, width), F32),
            pltpu.VMEM((n_ka * share, width), F32),
            pltpu.VMEM((n_ka, share, width), F32),
            pltpu.VMEM((n_ka, share, width), F32),
            dma((2, tiles)),
            dma(()),
            dma(()),
            dma(()),
            dma(()),
            dma((2, chunks)),
            dma((2, chunks)),
            dma((2, chunks)),
            dma((2, chunks)),
            dma((n_blocks,)),
            dma((n_blocks,)),
            dma((n_ka,)),
            dma((n_ka,)),
        ],
        compiler_params=pltpu.CompilerParams(
            collective_id=0, has_side_effects=True, vmem_limit_bytes=60 * 2**20
        ),
    )(basis_counts, moments, initial_vectors, final_vectors)
    return amplitude * amplitude


def solution(mesh):
    in_specs = (
        P(None, "vib", None),
        P("ka", "vib", "grp"),
        P("ka", "vib", ("grp", "fin")),
        P(("grp", "ka")),
    )
    out_specs = P(("grp", "ka", "vib"), "fin")
    return jax.shard_map(
        functools.partial(on_device, mesh.shape["ka"]),
        mesh=mesh, in_specs=in_specs, out_specs=out_specs, check_vma=False,
    )
```

time: 142 us -> 39.2 us (0.28)
  waiting for transfers between devices: 97.5 us -> 0 us
  Pallas kernels: 0 us -> 36.8 us
  matrix products: 17.5 us -> 0 us
  between operations: 13.5 us -> 0.01 us
  starting transfers between devices: 5.98 us -> 0 us
  local copies, waits for them, and re-layouts: 4.75 us -> 0 us
    psum x1 -> x0, waiting for transfers between devices: 58.5 us -> none  [on_device(): summed = lax.psum(amplitude, ('ka', 'vib'))]
    pallas_call x0 -> x1, Pallas kernels: none -> 36.8 us  [on_device(): pl.pallas_call(functools.partial(kernel, n_ka, chunks), out_shape=jax.Sha...]
    ppermute x2 -> x0, waiting for transfers between devices: 25.6 us -> none  [the longest x1 20.7 us: extended(): before = lax.ppermute(last, axis, up)]
    dot_general x2 -> x0, matrix products: 17.5 us -> none  [the longest x1 9.88 us: on_device(): jnp.einsum('kvi,vkf->if', initial_live.astype(jnp.float32), combined, pre...]
    all_gather x1 -> x0, waiting for transfers between devices: 13.4 us -> none  [on_device(): final_whole = lax.all_gather(final_live, 'vib', axis=1, tiled=True)]
    ppermute x2 -> x0, starting transfers between devices: 5.93 us -> none  [the longest x1 4.65 us: extended(): before = lax.ppermute(last, axis, up)]
    unnamed x5 -> x0, local copies, waits for them, and re-layouts: 3.29 us -> none
  transfers between devices with their start and end apart: 4 -> 0, of which waited for: 4 -> 0; matrix products, arithmetic and copies ran while one was open for 0% -> 0% of each run, Pallas kernels for 0% -> 0%
where the time goes in v1:
time: 39.2 us; the launch traced here: 38.5 us
  Pallas kernels  36.8 us (94%)
  other arithmetic  1.65 us (4%)
    pallas_call x1, Pallas kernels, on_device(): pl.pallas_call(functools.partial(kernel, n_ka, chunks), out_shape=jax.Sha...  36.8 us
    mul x1, other arithmetic, on_device(): return amplitude * amplitude  1.65 us

profile of v1, /device:TPU:0, one launch (start us, length us, event | category | flops | bytes accessed | tf_op | source)
XLA Modules:
  0.0 38.5 jit_solution(10306105276774715181)
XLA Ops:
  0.0 36.8 %shard_map.46 = f32[128,256]{1,0:T(8,128)} custom-call(s32[2]{0:T(128)} %counts_ref.1, bf16[2,1024,2048]{2,1,0:T(8,128)(2,1)} %moments_hbm.1, bf16[2,1024,1024]{2,1,0:T(8,128)(2,1)} %initial_hbm.1, bf16[2,1024,256]{2,1,0:T(8,128)(2,1)} %final_hbm.1), custom_call_target="tpu_custom_call" | custom-call | tf_op jit(solution)/shard_map/pallas_call | solution.py:281
  36.8 1.7 %mul.3 = f32[128,256]{1,0:T(8,128)} multiply(f32[128,256]{1,0:T(8,128)} %shard_map.46, f32[128,256]{1,0:T(8,128)} %shard_map.46) | non-fusion elementwise | flops 32768 | bytes 393216 | tf_op jit(solution)/shard_map/mul | solution.py:316

commit v2 on v1

v2 whole, which is shorter than its diff:
```python
import functools

import jax
import jax.numpy as jnp
from jax import lax
from jax.experimental import pallas as pl
from jax.experimental.pallas import tpu as pltpu
from jax.sharding import PartitionSpec as P

JQ = 30
MESH = pl.DeviceIdType.MESH
F32 = jnp.float32
BF16 = jnp.bfloat16


def coefficient_rows(index, width):
    value = jnp.full((1, width), index, jnp.int32).astype(F32)
    jsquare = float(JQ * (JQ + 1))
    norm_j = jnp.sqrt(jnp.full((1, width), jsquare, F32))
    same = value / norm_j
    upper = 0.5 * jnp.sqrt(jsquare - value * (value + 1.0)) / norm_j
    lower = -0.5 * jnp.sqrt(jsquare - value * (value - 1.0)) / norm_j
    return same, upper, lower


def kernel(
    n_ka, n_half, chunks, counts_ref, moments_hbm, initial_hbm, final_hbm, out_ref,
    mom, ini, raw, own, edge, comb, split, amp, part, zsend, zrecv,
    mom_sem, ini_sem, raw_sem, own_send, own_recv, z_send, z_recv,
    fwd_send, fwd_recv, part_send, part_recv, out_send, out_recv,
):
    kblocks, rows, width = raw.shape
    states = ini.shape[2]
    share = out_ref.shape[0]
    whole = mom.shape[2]
    half = width // n_half
    a = lax.axis_index("ka")
    b = lax.axis_index("vib")
    other = 1 - b
    first = a * kblocks - kblocks * n_ka // 2

    get_final = pltpu.make_async_copy(final_hbm, raw, raw_sem)
    get_final.start()
    cores = (b, other)

    def cols_of(core):
        return pl.ds(pl.multiple_of(core * rows, rows), rows)

    def get_moments(i, c):
        span = cols_of(cores[i])
        return pltpu.make_async_copy(
            moments_hbm.at[c, :, span], mom.at[c, :, span], mom_sem.at[i, c]
        )

    for i in range(2):
        for c in range(2):
            get_moments(i, c).start()
    get_initial = pltpu.make_async_copy(initial_hbm, ini, ini_sem)
    get_initial.start()

    barrier = pltpu.get_barrier_semaphore()
    pl.semaphore_signal(barrier, inc=1, device_id={"vib": other}, device_id_type=MESH)
    for d in range(1, n_ka):
        pl.semaphore_signal(
            barrier, inc=1, device_id={"ka": lax.rem(a + d, n_ka)}, device_id_type=MESH
        )

    get_final.wait()
    own_rows = cols_of(b)
    row_index = lax.broadcasted_iota(jnp.int32, (rows, half), 0) + b * rows
    for h in range(n_half):
        for k in range(kblocks):
            live = row_index < counts_ref[k]
            piece = raw[k, :, h * half : (h + 1) * half].astype(F32)
            own[h, own_rows, k * half : (k + 1) * half] = jnp.where(live, piece, 0.0).astype(BF16)

    has_up = a < n_ka - 1
    has_down = a > 0
    pl.semaphore_wait(barrier, n_ka)

    step = rows // chunks

    def at(core, j):
        return pl.ds(pl.multiple_of(core * rows + j * step, step), step)

    def side_lanes(side):
        return pl.ds(side * half, half)

    def z_copy(side, h, j):
        to = a + 1 if side == 0 else a - 1
        return pltpu.make_async_remote_copy(
            src_ref=own.at[h, at(b, j), side_lanes(1 - side)],
            dst_ref=edge.at[h, at(b, j), side_lanes(side)],
            send_sem=z_send.at[side, h, j],
            recv_sem=z_recv.at[side, h, j],
            device_id={"ka": to},
            device_id_type=MESH,
        )

    def forward(side, h, j):
        return pltpu.make_async_remote_copy(
            src_ref=edge.at[h, at(b, j), side_lanes(side)],
            dst_ref=edge.at[h, at(b, j), side_lanes(side)],
            send_sem=fwd_send.at[side, h, j],
            recv_sem=fwd_recv.at[side, h, j],
            device_id={"vib": other},
            device_id_type=MESH,
        )

    def own_copy(h):
        return pltpu.make_async_remote_copy(
            src_ref=own.at[h, own_rows],
            dst_ref=own.at[h, own_rows],
            send_sem=own_send.at[h],
            recv_sem=own_recv.at[h],
            device_id={"vib": other},
            device_id_type=MESH,
        )

    sends = (has_up, has_down)
    takes = (has_down, has_up)
    for h in range(n_half):
        for j in range(chunks):
            for side in range(2):
                @pl.when(sends[side])
                def _():
                    z_copy(side, h, j).start()
        own_copy(h).start()
    for side in range(2):
        @pl.when(jnp.logical_not(takes[side]))
        def _():
            for h in range(n_half):
                edge[h, :, side * half : (side + 1) * half] = jnp.zeros((whole, half), BF16)

    same0, upper0, _ = coefficient_rows(first, half)
    same1, _, lower1 = coefficient_rows(first + 1, half)
    _, upper_below, _ = coefficient_rows(first - 1, half)
    _, _, lower_above = coefficient_rows(first + 2, half)
    same_row = jnp.concatenate([same0, same1], axis=1)
    cross_row = jnp.concatenate([lower1, upper0], axis=1)
    edge_row = jnp.concatenate([upper_below, lower_above], axis=1)

    def relay(h, j):
        for side in range(2):
            @pl.when(takes[side])
            def _():
                z_copy(side, h, j).wait_recv()
                forward(side, h, j).start()

    tile = rows // 2
    for i in range(2):
        for c in range(2):
            get_moments(i, c).wait()
        for h in range(n_half):
            if i == 1:
                own_copy(h).wait_recv()
            piece = own[h, cols_of(cores[i]), :]
            for t in range(2):
                span = pl.ds(t * tile, tile)
                along_z = jnp.dot(
                    mom[0, span, cols_of(cores[i])], piece, preferred_element_type=F32
                )
                along_x = jnp.dot(
                    mom[1, span, cols_of(cores[i])], piece, preferred_element_type=F32
                )
                crossed = jnp.concatenate([along_x[:, half:], along_x[:, :half]], axis=1)
                value = same_row * along_z + cross_row * crossed
                comb[h, span, :] = value if i == 0 else comb[h, span, :] + value

    def take(h, core, j):
        piece = edge[h, at(core, j), :]
        for t in range(2):
            span = pl.ds(t * tile, tile)
            comb[h, span, :] = comb[h, span, :] + edge_row * jnp.dot(
                mom[1, span, at(core, j)], piece, preferred_element_type=F32
            )

    block = min(256, rows)
    lane_index = lax.broadcasted_iota(jnp.int32, (half, block), 1) + b * rows

    def split_half(h):
        for t in range(rows // block):
            both = comb[h, pl.ds(t * block, block), :].T
            for k in range(kblocks):
                turned = both[k * half : (k + 1) * half]
                turned = jnp.where(lane_index + t * block < counts_ref[k], turned, 0.0)
                high = turned.astype(BF16)
                low = (turned - high.astype(F32)).astype(BF16)
                split[h, k, pl.ds(0, half), pl.ds(t * block, block)] = high
                split[h, k, pl.ds(half, half), pl.ds(t * block, block)] = low

    lanes = min(256, states)
    n_blocks = states // lanes
    targets = lanes // (2 * share)
    own_block = a // targets if targets > 1 else a

    def block_of(s):
        return lax.rem(own_block + 1 + s, n_blocks)

    def part_copy(h, s):
        size = targets * share
        span = pl.ds(pl.multiple_of(block_of(s) * size, size), size)
        return pltpu.make_async_remote_copy(
            src_ref=amp.at[h, other, span],
            dst_ref=part.at[h, span],
            send_sem=part_send.at[h, s],
            recv_sem=part_recv.at[h, s],
            device_id={"vib": other},
            device_id_type=MESH,
        )

    def out_copy(h, target, slot):
        return pltpu.make_async_remote_copy(
            src_ref=zsend.at[h, slot],
            dst_ref=zrecv.at[h, a],
            send_sem=out_send.at[h, slot],
            recv_sem=out_recv.at[h, a],
            device_id={"ka": target},
            device_id_type=MESH,
        )

    def finish(h, s):
        part_copy(h, s).wait_recv()
        for j in range(targets):
            target = block_of(s) * targets + j
            span = pl.ds(pl.multiple_of(target * share, share), share)
            slot = s * targets + j
            value = amp[h, b, span, :] + part[h, span, :]
            zsend[h, slot] = value

            @pl.when(target == a)
            def _():
                out_ref[:, h * half : (h + 1) * half] = value

            @pl.when(target != a)
            def _():
                out_copy(h, target, slot).start()

    def amplitude_block(h, s):
        cols = pl.ds(pl.multiple_of(block_of(s) * lanes, lanes), lanes)
        both = jnp.dot(split[h, 0], ini[0, :, cols], preferred_element_type=F32)
        for k in range(1, kblocks):
            both = both + jnp.dot(split[h, k], ini[k, :, cols], preferred_element_type=F32)
        value = (both[:half] + both[half:]).T
        for j in range(targets):
            for core in range(2):
                low = (j * 2 + core) * share
                target = block_of(s) * targets + j
                amp[h, core, pl.ds(pl.multiple_of(target * share, share), share), :] = value[
                    low : low + share
                ]
        part_copy(h, s).start()

    for h in range(n_half):
        for j in range(chunks):
            if h == 0 or j > 0:
                relay(h, j)
            take(h, b, j)
        for j in range(chunks):
            for side in range(2):
                @pl.when(takes[side])
                def _():
                    forward(side, h, j).wait_recv()
            take(h, other, j)
        split_half(h)
        if h == 0:
            get_initial.wait()
        for s in range(n_blocks):
            amplitude_block(h, s)
            if s > 0:
                finish(h, s - 1)
            if s == n_blocks // 2 and h + 1 < n_half:
                relay(h + 1, 0)
    for h in range(n_half):
        finish(h, n_blocks - 1)

    for h in range(n_half):
        for d in range(1, n_ka):
            sender = lax.rem(a + d, n_ka)
            pltpu.make_async_remote_copy(
                src_ref=zsend.at[h, 0],
                dst_ref=zrecv.at[h, sender],
                send_sem=out_send.at[h, 0],
                recv_sem=out_recv.at[h, sender],
                device_id={"ka": sender},
                device_id_type=MESH,
            ).wait_recv()
            lanes_h = pl.ds(h * half, half)
            out_ref[:, lanes_h] = out_ref[:, lanes_h] + zrecv[h, sender]

    for h in range(n_half):
        own_copy(h).wait_send()
        for j in range(chunks):
            for side in range(2):
                @pl.when(sends[side])
                def _():
                    z_copy(side, h, j).wait_send()

                @pl.when(takes[side])
                def _():
                    forward(side, h, j).wait_send()
        for s in range(n_blocks):
            part_copy(h, s).wait_send()
            for j in range(targets):
                target = block_of(s) * targets + j

                @pl.when(target != a)
                def _():
                    out_copy(h, target, s * targets + j).wait_send()


def on_device(n_ka, moments, initial_vectors, final_vectors, basis_counts):
    kblocks, rows, states = initial_vectors.shape
    width = final_vectors.shape[2]
    whole = moments.shape[2]
    share = states // (2 * n_ka)
    n_half = max(1, width // 128)
    half = width // n_half
    chunks = 2
    dma = pltpu.SemaphoreType.DMA
    n_blocks = states // min(256, states)
    amplitude = pl.pallas_call(
        functools.partial(kernel, n_ka, n_half, chunks),
        out_shape=jax.ShapeDtypeStruct((share, width), F32),
        in_specs=[pl.BlockSpec(memory_space=pltpu.SMEM)]
        + [pl.BlockSpec(memory_space=pl.ANY)] * 3,
        out_specs=pl.BlockSpec(memory_space=pltpu.VMEM),
        scratch_shapes=[
            pltpu.VMEM(moments.shape, BF16),
            pltpu.VMEM(initial_vectors.shape, BF16),
            pltpu.VMEM(final_vectors.shape, BF16),
            pltpu.VMEM((n_half, whole, kblocks * half), BF16),
            pltpu.VMEM((n_half, whole, 2 * half), BF16),
            pltpu.VMEM((n_half, rows, kblocks * half), F32),
            pltpu.VMEM((n_half, kblocks, 2 * half, rows), BF16),
            pltpu.VMEM((n_half, 2, n_ka * share, half), F32),
            pltpu.VMEM((n_half, n_ka * share, half), F32),
            pltpu.VMEM((n_half, n_ka, share, half), F32),
            pltpu.VMEM((n_half, n_ka, share, half), F32),
            dma((2, 2)),
            dma(()),
            dma(()),
            dma((n_half,)),
            dma((n_half,)),
            dma((2, n_half, chunks)),
            dma((2, n_half, chunks)),
            dma((2, n_half, chunks)),
            dma((2, n_half, chunks)),
            dma((n_half, n_blocks)),
            dma((n_half, n_blocks)),
            dma((n_half, n_ka)),
            dma((n_half, n_ka)),
        ],
        compiler_params=pltpu.CompilerParams(
            collective_id=0, has_side_effects=True, vmem_limit_bytes=60 * 2**20
        ),
    )(basis_counts, moments, initial_vectors, final_vectors)
    return amplitude * amplitude


def solution(mesh):
    in_specs = (
        P(None, "vib", None),
        P("ka", "vib", "grp"),
        P("ka", "vib", ("grp", "fin")),
        P(("grp", "ka")),
    )
    out_specs = P(("grp", "ka", "vib"), "fin")
    return jax.shard_map(
        functools.partial(on_device, mesh.shape["ka"]),
        mesh=mesh, in_specs=in_specs, out_specs=out_specs, check_vma=False,
    )
```

time: 39.2 us -> 32.9 us (0.84); the launches traced: 38.5 us -> 32.8 us
  Pallas kernels: 36.8 us -> 31.1 us
    pallas_call x1, Pallas kernels: 36.8 us -> 31.1 us  [on_device(): pl.pallas_call(functools.partial(kernel, n_ka, n_half, chunks), out_shape...]
where the time goes in v2:
time: 32.9 us; the launch traced here: 32.8 us
  Pallas kernels  31.1 us (95%)
  other arithmetic  1.65 us (5%)
    pallas_call x1, Pallas kernels, on_device(): pl.pallas_call(functools.partial(kernel, n_ka, n_half, chunks), out_shape...  31.1 us
    mul x1, other arithmetic, on_device(): return amplitude * amplitude  1.65 us

profile of v2, /device:TPU:0, one launch (start us, length us, event | category | flops | bytes accessed | tf_op | source)
XLA Modules:
  0.0 32.8 jit_solution(12738087804770993237)
XLA Ops:
  0.0 31.1 %shard_map.46 = f32[128,256]{1,0:T(8,128)} custom-call(s32[2]{0:T(128)} %counts_ref.1, bf16[2,1024,2048]{2,1,0:T(8,128)(2,1)} %moments_hbm.1, bf16[2,1024,1024]{2,1,0:T(8,128)(2,1)} %initial_hbm.1, bf16[2,1024,256]{2,1,0:T(8,128)(2,1)} %final_hbm.1), custom_call_target="tpu_custom_call" | custom-call | tf_op jit(solution)/shard_map/pallas_call | solution.py:322
  31.1 1.7 %mul.3 = f32[128,256]{1,0:T(8,128)} multiply(f32[128,256]{1,0:T(8,128)} %shard_map.46, f32[128,256]{1,0:T(8,128)} %shard_map.46) | non-fusion elementwise | flops 32768 | bytes 393216 | tf_op jit(solution)/shard_map/mul | solution.py:358

commit v3 on v2

--- a/solution.py
+++ b/solution.py
@@ -194,8 +194,10 @@
     targets = lanes // (2 * share)
     own_block = a // targets if targets > 1 else a
 
+    toward = 2 * ((2 * a) // n_ka) - 1
+
     def block_of(s):
-        return lax.rem(own_block + 1 + s, n_blocks)
+        return lax.rem(own_block + toward * (1 + s) + n_blocks, n_blocks)
 
     def part_copy(h, s):
         size = targets * share

time: 32.9 us -> 32.5 us (0.988)
  Pallas kernels: 31.1 us -> 30.7 us
    pallas_call x1, Pallas kernels: 31.1 us -> 30.7 us  [on_device(): pl.pallas_call(functools.partial(kernel, n_ka, n_half, chunks), out_shape...]
where the time goes in v3:
time: 32.5 us; the launch traced here: 32.3 us
  Pallas kernels  30.7 us (94%)
  other arithmetic  1.65 us (5%)
    pallas_call x1, Pallas kernels, on_device(): pl.pallas_call(functools.partial(kernel, n_ka, n_half, chunks), out_shape...  30.7 us
    mul x1, other arithmetic, on_device(): return amplitude * amplitude  1.65 us

profile of v3, /device:TPU:0, one launch (start us, length us, event | category | flops | bytes accessed | tf_op | source)
XLA Modules:
  0.0 32.3 jit_solution(18351532081021488222)
XLA Ops:
  0.0 30.7 %shard_map.46 = f32[128,256]{1,0:T(8,128)} custom-call(s32[2]{0:T(128)} %counts_ref.1, bf16[2,1024,2048]{2,1,0:T(8,128)(2,1)} %moments_hbm.1, bf16[2,1024,1024]{2,1,0:T(8,128)(2,1)} %initial_hbm.1, bf16[2,1024,256]{2,1,0:T(8,128)(2,1)} %final_hbm.1), custom_call_target="tpu_custom_call" | custom-call | tf_op jit(solution)/shard_map/pallas_call | solution.py:324
  30.7 1.7 %mul.3 = f32[128,256]{1,0:T(8,128)} multiply(f32[128,256]{1,0:T(8,128)} %shard_map.46, f32[128,256]{1,0:T(8,128)} %shard_map.46) | non-fusion elementwise | flops 32768 | bytes 393216 | tf_op jit(solution)/shard_map/mul | solution.py:360
